TPU v7x, 256 devices: a whole 4x4x8 slice. The times are simulated.
256 devices in a mesh: grp: 8 (over z_hi, core), dev: 32 (over y, x, z_lo).
Axes of the slice: x: 4, y: 4, z: 8 (z_hi: 4, z_lo: 2; z = z_hi * 2 + z_lo), core: 2. Of those that a mesh axis runs over, the one named last changes fastest.
Arguments:
- queries: float32 [256, 12, 128], P(('grp', 'dev')), may hold values from -2.1 to 2.1
- pages: float32 [256, 256, 128], P(('grp', 'dev')), may hold values from -2.1 to 2.1
- positive: int32 [256], replicated, may hold values from 0 to 255
Outputs:
- loss: float32 [], replicated
- question_token_slope: float32 [256, 12, 128], P(('grp', 'dev'))
- page_grad: float32 [256, 256, 128], P(('grp', 'dev'))
All inputs are finite; a program needn't handle non-finite values.
Results may differ from a plain program's by a relative error of at most 0.00019.
Values sent between devices are 32-bit elements; how exact they have to be, the bound alone decides.
No kernel may reach another device: no remote copies, remote signals or barrier semaphores. Data moves between devices by JAX's collectives and lax.ppermute only.
A program may use at most 64 MiB of HBM per device.

v0:
```python
import functools
import jax
import jax.numpy as jnp
from jax import lax
from jax.sharding import Mesh
from jax.sharding import PartitionSpec as P

GRP_DEV = ("grp_0", "grp_1", "dev_0", "dev_1", "dev_2")
cap_value = 4.0
sharpness_divisor = 0.25
logit_scale = 8.0
z_weight = 0.001
highest = lax.Precision.HIGHEST


def one_axis_at_a_time(shard, axes):
    return functools.reduce(lax.psum, axes, shard)


def block_partial_terms(query_rows, page_rows, query_tokens):
    scores = jnp.dot(query_rows, page_rows.T, precision=highest, preferred_element_type=jnp.float32)
    tangent = jnp.tanh(scores / cap_value)
    bounded_similarity = cap_value * tangent
    exponential_grid = jnp.exp(bounded_similarity / sharpness_divisor)
    accumulated_totals = jnp.sum(exponential_grid, axis=1)
    gentle_peak = sharpness_divisor * jnp.log(accumulated_totals)
    slopes = (
        exponential_grid
        / accumulated_totals[:, None]
        * (1.0 - tangent * tangent)
        * (logit_scale / query_tokens)
    )
    return (gentle_peak, slopes)


def shards(queries, pages, positive):
    gathered = lax.all_gather(queries, GRP_DEV, axis=0, tiled=True)
    query_count, query_tokens, feature_width = gathered.shape
    page_rows = pages[0]
    page_index = lax.axis_index(GRP_DEV)
    block_size = 16
    block_count = query_count // block_size
    query_blocks = gathered.reshape(block_count, block_size * query_tokens, feature_width)
    chosen = (positive == page_index).astype(jnp.float32)

    def block_logits(gentle_peak):
        return (
            logit_scale / query_tokens * gentle_peak.reshape(block_size, query_tokens).sum(axis=1)
        )

    def evaluate_loss_and_slopes(query_rows):
        gentle_peak, slopes = block_partial_terms(query_rows, page_rows, query_tokens)
        unscaled = jnp.dot(slopes, page_rows, precision=highest, preferred_element_type=jnp.float32)
        return (block_logits(gentle_peak), unscaled)

    logits, unscaled = lax.map(evaluate_loss_and_slopes, query_blocks)
    statistics_logits = logits.reshape(query_count)
    exponential_grid = jnp.exp(statistics_logits)
    accumulated_totals = one_axis_at_a_time(exponential_grid, GRP_DEV)
    matching_logit = one_axis_at_a_time(chosen * statistics_logits, GRP_DEV)
    log_totals = jnp.log(accumulated_totals)
    loss = jnp.mean(log_totals - matching_logit + z_weight * log_totals * log_totals)
    coefficients = (
        (1.0 + 2.0 * z_weight * log_totals) * exponential_grid / accumulated_totals - chosen
    ) / query_count
    loss, coefficients = (loss, coefficients)
    factors = jnp.repeat(coefficients, query_tokens).reshape(
        block_count, block_size * query_tokens, 1
    )
    query_terms = unscaled * factors

    def page_only(page_total, inputs):
        query_rows, factor_rows = inputs
        unused_smooth, slopes = block_partial_terms(query_rows, page_rows, query_tokens)
        token_grads = slopes * factor_rows
        page_total = page_total + jnp.dot(
            token_grads.T, query_rows, precision=highest, preferred_element_type=jnp.float32
        )
        return (page_total, None)

    page_start = jnp.zeros(page_rows.shape, jnp.float32)
    page_total, unused_outputs = lax.scan(page_only, page_start, (query_blocks, factors))
    query_terms = query_terms.reshape(query_count, query_tokens, feature_width)
    summed = lax.psum(query_terms, GRP_DEV)
    own_count = queries.shape[0]
    question_token_slope = lax.dynamic_slice_in_dim(summed, page_index * own_count, own_count, 0)
    return (loss, question_token_slope, page_total[None])


def solution(mesh):
    finer = Mesh(mesh.devices.reshape(4, 2, 4, 4, 2), ("grp_0", "grp_1", "dev_0", "dev_1", "dev_2"))
    placed = (P(GRP_DEV, None, None), P(GRP_DEV, None, None), P())
    return jax.shard_map(
        shards,
        mesh=finer,
        in_specs=placed,
        out_specs=(P(), P(GRP_DEV, None, None), P(GRP_DEV, None, None)),
        check_vma=False,
    )
```

profile of v0, /device:TPU:2, one launch (start us, length us, event | category | flops | bytes accessed | tf_op | source)
XLA Modules:
  0.0 1047.5 jit_solution(13401674488803938812)
XLA Ops:
  7.2 1.3 copy.13
  8.6 696.5 %all-gather.2.cloned.1.call-done = f32[256,12,128]{2,1,0:T(8,128)} async-done(((f32[1,12,128]{2,1,0:T(8,128)}), f32[256,12,128]{2,1,0:T(8,128)}) %all-gather.2.cloned.1.call-update) | async-done | bytes 1572880 | tf_op jit(solution)/shard_map/all_gather | solution.py:37
  705.1 1.6 reshape.45
  706.7 27.7 %while.27 = (s32[]{:T(128)}, f32[16,16]{1,0:T(8,128)S(1)}, f32[16,192,128]{2,1,0:T(8,128)}, f32[16,192,128]{2,1,0:T(8,128)S(1)}, f32[256,128]{1,0:T(8,128)S(1)}, /*index=5*/s32[]{:T(128)}, f32[]{:T(128)}, s32[]{:T(128)}) while((s32[]{:T(128)}, f32[16,16]{1,0:T(8,128)S(1)}, f32[16,192,128]{2,1,0:T(8,128)}, f32[16,192,128]{2,1,0:T(8,128)S(1)}, ...), condition=%wide.region_3.4_spmd, body=%wide.region_0.3_spmd.sunk | while | flops 151437504 | bytes 857773 | solution.py:56
  707.5 1.0 fusion.56
  709.2 1.0 fusion.56
  710.9 1.0 fusion.56
  712.7 1.0 fusion.56
  714.4 1.0 fusion.56
  716.1 1.0 fusion.56
  717.8 1.0 fusion.56
  719.6 1.0 fusion.56
  721.3 1.0 fusion.56
  723.0 1.0 fusion.56
  724.8 1.0 fusion.56
  726.5 1.0 fusion.56
  728.2 1.0 fusion.56
  730.0 1.0 fusion.56
  731.7 1.0 fusion.56
  733.4 1.0 fusion.56
  734.5 15.1 %all-reduce.2 = (f32[256]{0:T(256)S(1)}, f32[256]{0:T(256)S(1)}) all-reduce(f32[256]{0:T(256)S(1)} %get-tuple-element.216, f32[256]{0:T(256)S(1)} %get-tuple-element.215), channel_id=1, replica_groups=mesh['grp_0'=4,'grp_1'=2,'dev_0'=4,'dev_1'=4,'dev_2'=2] {'grp_0'}, use_global_device_ids=true, to_apply=%region_9.10 | all-reduce | flops 512 | bytes 4096 | tf_op jit(solution)/shard_map/psum | solution.py:17
  749.7 2.4 all-reduce.4
  752.1 7.7 all-reduce.1
  759.8 9.2 all-reduce
  769.0 6.2 all-reduce.3
  775.2 0.6 subtract_multiply_fusion
  776.2 1.9 broadcast_multiply_fusion
  778.1 1.4 reshape.47
  779.6 0.9 copy-done.2
  780.4 20.1 %while.28 = (s32[]{:T(128)}, f32[256,128]{1,0:T(8,128)S(1)}, f32[16,192,128]{2,1,0:T(8,128)S(1)}, f32[256,128]{1,0:T(8,128)S(1)}, f32[16,192,1]{1,2,0:T(1,128)S(1)}, /*index=5*/s32[]{:T(128)}, s32[]{:T(128)}) while((s32[]{:T(128)}, f32[256,128]{1,0:T(8,128)S(1)}, f32[16,192,128]{2,1,0:T(8,128)S(1)}, f32[256,128]{1,0:T(8,128)S(1)}, ...), condition=%wide.region_18.19_spmd.clone, body=%wide.region_16.18_spmd.clone.sunk | while | flops 151502848 | bytes 987499 | solution.py:82
  780.9 0.8 convolution_add_fusion.2
  781.7 0.5 fusion.60
  782.1 0.8 convolution_add_fusion.2
  783.0 0.5 fusion.60
  783.4 0.8 convolution_add_fusion.2
  784.2 0.5 fusion.60
  784.7 0.8 convolution_add_fusion.2
  785.5 0.5 fusion.60
  785.9 0.8 convolution_add_fusion.2
  786.7 0.5 fusion.60
  787.2 0.8 convolution_add_fusion.2
  788.0 0.5 fusion.60
  788.5 0.8 convolution_add_fusion.2
  789.3 0.5 fusion.60
  789.7 0.8 convolution_add_fusion.2
  790.5 0.5 fusion.60
  791.0 0.8 convolution_add_fusion.2
  791.8 0.5 fusion.60
  792.2 0.8 convolution_add_fusion.2
  793.0 0.5 fusion.60
  793.5 0.8 convolution_add_fusion.2
  794.3 0.5 fusion.60
  794.8 0.8 convolution_add_fusion.2
  795.6 0.5 fusion.60
  796.0 0.8 convolution_add_fusion.2
  796.8 0.5 fusion.60
  797.3 0.8 convolution_add_fusion.2
  798.1 0.5 fusion.60
  798.5 0.8 convolution_add_fusion.2
  799.3 0.5 fusion.60
  799.8 0.8 convolution_add_fusion.2
  801.2 237.0 %all-reduce.7.cloned.1.call-done = f32[256,12,128]{2,1,0:T(8,128)} async-done(((f32[256,12,128]{2,1,0:T(8,128)}), f32[256,12,128]{2,1,0:T(8,128)}) %all-reduce.7.cloned.1.call-update) | async-done | bytes 1572880 | tf_op jit(solution)/shard_map/psum | solution.py:84
  1038.3 0.7 constant_dynamic-slice_fusion
  1039.0 0.6 copy.15
  (133 shorter events, 12.3 us)
Async XLA Ops:
  7.2 697.9 %all-gather.2.cloned.1.call-start = ((), (), s32[]{:S(2)}) async-start(), calls=%async_computation | async-start | bytes 2105344 | tf_op jit(solution)/shard_map/all_gather | solution.py:37
  8.5 1029.7 %all-reduce.7.cloned.1.call-start = ((), (), s32[]{:S(2)}) async-start(), calls=%async_computation.1 | async-start | bytes 4194304 | tf_op jit(solution)/shard_map/psum | solution.py:84
  8.6 698.1 %copy-start = (f32[1,256,128]{2,1,0:T(8,128)S(1)}, f32[1,256,128]{2,1,0:T(8,128)}, u32[]{:S(2)}) copy-start(f32[1,256,128]{2,1,0:T(8,128)} %param.8) | copy-start | bytes 393220
  706.7 27.8 %copy-start.1 = (s32[256]{0:T(256)S(1)}, s32[256]{0:T(256)}, u32[]{:S(2)}) copy-start(s32[256]{0:T(256)} %param.9) | copy-start | bytes 3076
  779.5 0.9 copy-start.2
  800.6 239.0 %copy-start.3 = (f32[256,128]{1,0:T(8,128)}, f32[256,128]{1,0:T(8,128)S(1)}, u32[]{:S(2)}) copy-start(f32[256,128]{1,0:T(8,128)S(1)} %get-tuple-element.136) | copy-start | bytes 393220
Sparse Core Ops, SparseCore 0:
  9.9 695.1 all-gather.1
  779.7 258.5 all-reduce.6
where the time goes:
time: 1050 us
  waiting for transfers between devices  934 us (89%)
  matrix products  42.8 us (4%)
  blocking collectives  40.6 us (4%)
  between operations  15.9 us (2%)
    all_gather x1, waiting for transfers between devices, shards(): gathered = lax.all_gather(queries, GRP_DEV, axis=0, tiled=True)  696 us
    psum x1, waiting for transfers between devices, shards(): summed = lax.psum(query_terms, GRP_DEV)  237 us
    psum x5, blocking collectives, one_axis_at_a_time(): return functools.reduce(lax.psum, axes, shard)  40.6 us
  transfers between devices with their start and end apart: 2, of which 2 were waited for; matrix products, arithmetic and copies ran while one was open for 2% of the time, Pallas kernels for 0%

commit v1 on v0

--- a/solution.py
+++ b/solution.py
@@ -34,7 +34,8 @@
 
 
 def shards(queries, pages, positive):
-    gathered = lax.all_gather(queries, GRP_DEV, axis=0, tiled=True)
+    outgoing = jnp.stack([queries] * lax.axis_size(GRP_DEV))
+    gathered = jnp.concatenate(lax.all_to_all(outgoing, GRP_DEV, 0, 0), axis=0)
     query_count, query_tokens, feature_width = gathered.shape
     page_rows = pages[0]
     page_index = lax.axis_index(GRP_DEV)

time: 1050 us -> 401 us (0.38)
  waiting for transfers between devices: 934 us -> 277 us
  starting transfers between devices: 0.08 us -> 14.7 us
    all_gather x1 -> x0, waiting for transfers between devices: 696 us -> none  [shards(): gathered = lax.all_gather(queries, GRP_DEV, axis=0, tiled=True)]
    all_to_all x0 -> x1, waiting for transfers between devices: none -> 41.5 us  [shards(): gathered = jnp.concatenate(lax.all_to_all(outgoing, GRP_DEV, 0, 0), axis=0)]
    all_to_all x0 -> x1, starting transfers between devices: none -> 14.7 us  [shards(): gathered = jnp.concatenate(lax.all_to_all(outgoing, GRP_DEV, 0, 0), axis=0)]
  transfers between devices with their start and end apart: 2 -> 2, of which waited for: 2 -> 2; matrix products, arithmetic and copies ran while one was open for 2% -> 5% of each run, Pallas kernels for 0% -> 0%
where the time goes in v1:
time: 401 us
  waiting for transfers between devices  277 us (69%)
  matrix products  42.8 us (11%)
  blocking collectives  35.9 us (9%)
  between operations  15.9 us (4%)
  starting transfers between devices  14.7 us (4%)
  local copies, waits for them, and re-layouts  8.65 us (2%)
  other arithmetic  4.71 us (1%)
    psum x1, waiting for transfers between devices, shards(): summed = lax.psum(query_terms, GRP_DEV)  235 us
    all_to_all x1, waiting for transfers between devices, shards(): gathered = jnp.concatenate(lax.all_to_all(outgoing, GRP_DEV, 0, 0), axis=0)  41.5 us
    psum x5, blocking collectives, one_axis_at_a_time(): return functools.reduce(lax.psum, axes, shard)  35.9 us
    dot_general x16, matrix products, evaluate_loss_and_slopes(): jnp.dot(slopes, page_rows, precision=highest, preferred_element_type=jnp....  16.1 us
    all_to_all x1, starting transfers between devices, shards(): gathered = jnp.concatenate(lax.all_to_all(outgoing, GRP_DEV, 0, 0), axis=0)  14.7 us
    dot_general x32, matrix products, block_partial_terms(): jnp.dot(query_rows, page_rows.T, precision=highest, preferred_element_typ...  14.4 us
    dot_general x16, matrix products, page_only(): jnp.dot(token_grads.T, query_rows, precision=highest, preferred_element_t...  12.3 us
  transfers between devices with their start and end apart: 2, of which 2 were waited for; matrix products, arithmetic and copies ran while one was open for 5% of the time, Pallas kernels for 0%

profile of v1, /device:TPU:2, one launch (start us, length us, event | category | flops | bytes accessed | tf_op | source)
XLA Modules:
  0.0 400.6 jit_solution(17615402208355352727)
XLA Ops:
  7.2 0.7 copy.14
  7.9 2.0 stack.2
  9.8 14.7 %all-to-all-start = ((f32[256,1,12,128]{3,1,2,0:T(1,128)}), f32[256,1,12,128]{3,1,2,0:T(1,128)S(1)}, u32[]{:S(2)}, u32[]{:S(2)}) async-start(f32[256,1,12,128]{3,1,2,0:T(1,128)} %stack.2), calls=%async_computation | async-start | bytes 3145728 | tf_op jit(solution)/shard_map/all_to_all | solution.py:38
  24.6 41.5 %all-to-all-done = f32[256,1,12,128]{3,1,2,0:T(1,128)S(1)} async-done(((f32[256,1,12,128]{3,1,2,0:T(1,128)}), f32[256,1,12,128]{3,1,2,0:T(1,128)S(1)}, u32[]{:S(2)}, u32[]{:S(2)}) %all-to-all-start) | async-done | bytes 1572896 | tf_op jit(solution)/shard_map/all_to_all | solution.py:38
  66.2 27.7 %while.27 = (s32[]{:T(128)}, f32[16,16]{1,0:T(8,128)S(1)}, f32[16,192,128]{2,1,0:T(8,128)}, f32[16,192,128]{2,1,0:T(8,128)S(1)}, f32[256,128]{1,0:T(8,128)S(1)}, /*index=5*/s32[]{:T(128)}, f32[]{:T(128)}, s32[]{:T(128)}) while((s32[]{:T(128)}, f32[16,16]{1,0:T(8,128)S(1)}, f32[16,192,128]{2,1,0:T(8,128)}, f32[16,192,128]{2,1,0:T(8,128)S(1)}, ...), condition=%wide.region_3.4_spmd, body=%wide.region_0.3_spmd.sunk | while | flops 151437504 | bytes 857773 | solution.py:57
  66.9 1.0 fusion.56
  68.6 1.0 fusion.56
  70.3 1.0 fusion.56
  72.1 1.0 fusion.56
  73.8 1.0 fusion.56
  75.5 1.0 fusion.56
  77.3 1.0 fusion.56
  79.0 1.0 fusion.56
  80.7 1.0 fusion.56
  82.5 1.0 fusion.56
  84.2 1.0 fusion.56
  85.9 1.0 fusion.56
  87.7 1.0 fusion.56
  89.4 1.0 fusion.56
  91.1 1.0 fusion.56
  92.9 1.0 fusion.56
  94.0 10.2 %all-reduce.2 = (f32[256]{0:T(256)S(1)}, f32[256]{0:T(256)S(1)}) all-reduce(f32[256]{0:T(256)S(1)} %get-tuple-element.216, f32[256]{0:T(256)S(1)} %get-tuple-element.215), channel_id=1, replica_groups=mesh['grp_0'=4,'grp_1'=2,'dev_0'=4,'dev_1'=4,'dev_2'=2] {'grp_0'}, use_global_device_ids=true, to_apply=%region_9.10 | all-reduce | flops 512 | bytes 4096 | tf_op jit(solution)/shard_map/psum | solution.py:17
  104.2 2.4 all-reduce.4
  106.6 9.2 %all-reduce.1 = (f32[256]{0:T(256)S(1)}, f32[256]{0:T(256)S(1)}) all-reduce(f32[256]{0:T(256)S(1)} %get-tuple-element.207, f32[256]{0:T(256)S(1)} %get-tuple-element.208), channel_id=1, replica_groups=mesh['grp_0'=4,'grp_1'=2,'dev_0'=4,'dev_1'=4,'dev_2'=2] {'dev_0'}, use_global_device_ids=true, to_apply=%region_11.12 | all-reduce | flops 512 | bytes 4096 | tf_op jit(solution)/shard_map/psum | solution.py:17
  115.8 9.1 %all-reduce = (f32[256]{0:T(256)S(1)}, f32[256]{0:T(256)S(1)}) all-reduce(f32[256]{0:T(256)S(1)} %get-tuple-element.201, f32[256]{0:T(256)S(1)} %get-tuple-element.202), channel_id=1, replica_groups=mesh['grp_0'=4,'grp_1'=2,'dev_0'=4,'dev_1'=4,'dev_2'=2] {'dev_1'}, use_global_device_ids=true, to_apply=%region_12.13 | all-reduce | flops 512 | bytes 4096 | tf_op jit(solution)/shard_map/psum | solution.py:17
  124.9 4.9 %all-reduce.3 = (f32[256]{0:T(256)S(1)}, f32[256]{0:T(256)S(1)}) all-reduce(f32[256]{0:T(256)S(1)} %get-tuple-element.199, f32[256]{0:T(256)S(1)} %get-tuple-element.200), channel_id=1, replica_groups=mesh['grp_0'=4,'grp_1'=2,'dev_0'=4,'dev_1'=4,'dev_2'=2] {'dev_2'}, use_global_device_ids=true, to_apply=%region_13.14 | all-reduce | flops 512 | bytes 4096 | tf_op jit(solution)/shard_map/psum | solution.py:17
  129.9 0.6 subtract_multiply_fusion
  130.9 1.9 broadcast_multiply_fusion
  132.8 1.4 reshape.46
  134.2 0.9 copy-done.2
  135.1 20.1 %while.28 = (s32[]{:T(128)}, f32[256,128]{1,0:T(8,128)S(1)}, f32[16,192,128]{2,1,0:T(8,128)S(1)}, f32[256,128]{1,0:T(8,128)S(1)}, f32[16,192,1]{1,2,0:T(1,128)S(1)}, /*index=5*/s32[]{:T(128)}, s32[]{:T(128)}) while((s32[]{:T(128)}, f32[256,128]{1,0:T(8,128)S(1)}, f32[16,192,128]{2,1,0:T(8,128)S(1)}, f32[256,128]{1,0:T(8,128)S(1)}, ...), condition=%wide.region_18.19_spmd.clone, body=%wide.region_16.18_spmd.clone.sunk | while | flops 151502848 | bytes 987499 | solution.py:83
  135.6 0.8 convolution_add_fusion.2
  136.4 0.5 fusion.60
  136.8 0.8 convolution_add_fusion.2
  137.6 0.5 fusion.60
  138.1 0.8 convolution_add_fusion.2
  138.9 0.5 fusion.60
  139.3 0.8 convolution_add_fusion.2
  140.2 0.5 fusion.60
  140.6 0.8 convolution_add_fusion.2
  141.4 0.5 fusion.60
  141.9 0.8 convolution_add_fusion.2
  142.7 0.5 fusion.60
  143.1 0.8 convolution_add_fusion.2
  143.9 0.5 fusion.60
  144.4 0.8 convolution_add_fusion.2
  145.2 0.5 fusion.60
  145.6 0.8 convolution_add_fusion.2
  146.5 0.5 fusion.60
  146.9 0.8 convolution_add_fusion.2
  147.7 0.5 fusion.60
  148.2 0.8 convolution_add_fusion.2
  149.0 0.5 fusion.60
  149.4 0.8 convolution_add_fusion.2
  150.2 0.5 fusion.60
  150.7 0.8 convolution_add_fusion.2
  151.5 0.5 fusion.60
  151.9 0.8 convolution_add_fusion.2
  152.8 0.5 fusion.60
  153.2 0.8 convolution_add_fusion.2
  154.5 0.8 convolution_add_fusion.2
  155.9 235.4 %all-reduce.7.cloned.1.call-done = f32[256,12,128]{2,1,0:T(8,128)} async-done(((f32[256,12,128]{2,1,0:T(8,128)}), f32[256,12,128]{2,1,0:T(8,128)}) %all-reduce.7.cloned.1.call-update) | async-done | bytes 1572880 | tf_op jit(solution)/shard_map/psum | solution.py:85
  391.3 0.7 constant_dynamic-slice_fusion
  392.0 0.6 copy.11
  (132 shorter events, 12.7 us)
Async XLA Ops:
  9.8 56.3 %copy-start = (f32[1,256,128]{2,1,0:T(8,128)S(1)}, f32[1,256,128]{2,1,0:T(8,128)}, u32[]{:S(2)}) copy-start(f32[1,256,128]{2,1,0:T(8,128)} %param.8) | copy-start | bytes 393220
  9.8 56.3 %all-to-all-start = ((f32[256,1,12,128]{3,1,2,0:T(1,128)}), f32[256,1,12,128]{3,1,2,0:T(1,128)S(1)}, u32[]{:S(2)}, u32[]{:S(2)}) async-start(f32[256,1,12,128]{3,1,2,0:T(1,128)} %stack.2), calls=%async_computation | async-start | bytes 3145728 | tf_op jit(solution)/shard_map/all_to_all | solution.py:38
  24.5 366.8 %all-reduce.7.cloned.1.call-start = ((), (), s32[]{:S(2)}) async-start(), calls=%async_computation.1 | async-start | bytes 4194304 | tf_op jit(solution)/shard_map/psum | solution.py:85
  66.2 27.8 %copy-start.1 = (s32[256]{0:T(256)S(1)}, s32[256]{0:T(256)}, u32[]{:S(2)}) copy-start(s32[256]{0:T(256)} %param.9) | copy-start | bytes 3076
  134.2 0.9 copy-start.2
  155.3 237.4 %copy-start.3 = (f32[256,128]{1,0:T(8,128)}, f32[256,128]{1,0:T(8,128)S(1)}, u32[]{:S(2)}) copy-start(f32[256,128]{1,0:T(8,128)S(1)} %get-tuple-element.136) | copy-start | bytes 393220
Sparse Core Ops, SparseCore 0:
  134.4 256.9 all-reduce.6
